TPU v7x, 256 devices: a whole 4x4x8 slice. The times are simulated.
256 devices in a mesh: panel: 16 (over x, y), front: 16 (over z, core).
Axes of the slice: x: 4, y: 4, z: 8, core: 2. Of those that a mesh axis runs over, the one named last changes fastest.
Arguments:
- leaf_inv: float32 [16, 16, 768, 768], P('panel', 'front'), may hold values from -0.21875 to 0.21875
- parent_inv: float32 [16, 16, 768, 768], P('panel', 'front'), may hold values from -0.21875 to 0.21875
- up_coupling: float32 [16, 16, 384, 768], P('panel', 'front'), may hold values from -0.21875 to 0.21875
- down_coupling: float32 [16, 16, 768, 384], P('panel', 'front'), may hold values from -0.3125 to 0.3125
- interface_coupling: float32 [16, 16, 768, 512], P('panel', 'front'), may hold values from -0.25 to 0.25
- leaf_sources: float32 [16, 16, 3, 768, 128], P('panel', 'front'), may hold values from -6 to 6
- parent_sources: float32 [16, 16, 3, 768, 128], P('panel', 'front'), may hold values from -6 to 6
- parent_of: int32 [16, 16], P('panel'), may hold values from 0 to 15
- update_count: int32 [16, 16], P('panel'), may hold values from 128 to 384, as said below
- update_rows: int32 [16, 16, 384], P('panel'), may hold values from 0 to 767, as said below
Outputs:
- leaf_solution: float32 [16, 16, 3, 768, 128], P('panel', 'front')
- parent_solution: float32 [16, 16, 3, 768, 128], P('panel', 'front')
Inputs may be any that keep to these rules, and one draw needn't show every extreme that they name: `update_count`: a multiple of 128; some leaf of every panel has 384. `update_rows`: the entries of one leaf are distinct; those at or past its update_count are padding.
All inputs are finite; a program needn't handle non-finite values.
Results may differ from a plain program's by a relative error of at most 0.0003.
Values sent between devices are 32-bit elements; how exact they have to be, the bound alone decides.
A program may use at most 128 MiB of HBM per device.

v0:
```python
import jax
import jax.numpy as jnp
from jax import lax
from jax.sharding import PartitionSpec as P

TICKS = 3
highest_precision = lax.Precision.HIGHEST


def passed_along(value, axis, steps):
    count = lax.axis_size(axis)
    leading, last = (max(0, -steps), min(count, count - steps))
    return lax.ppermute(value, axis, [(source, source + steps) for source in range(leading, last)])


def product(matrix, operand):
    return jnp.dot(matrix, operand, precision=highest_precision, preferred_element_type=jnp.float32)


def local(
    leaf_inv,
    parent_inv,
    up_coupling,
    down_coupling,
    interface_coupling,
    leaf_sources,
    parent_sources,
    parent_of,
    update_count,
    update_rows,
):
    inverse = leaf_inv[0, 0]
    parent_inverse = parent_inv[0, 0]
    upward = up_coupling[0, 0]
    downward = down_coupling[0, 0]
    coupling = interface_coupling[0, 0]
    leaf_order = inverse.shape[0]
    parent_order = parent_inverse.shape[0]
    iface_rows = coupling.shape[1]
    parents = parent_of[0]
    counts = update_count[0]
    row_ids = update_rows[0]
    update_cap = row_ids.shape[1]
    myself = lax.axis_index("front")
    slot_ids = jnp.arange(update_cap, dtype=jnp.int32)[None, :]
    live_slots = slot_ids < counts[:, None]
    mine = live_slots & (parents[:, None] == myself)
    targets = jnp.where(mine, row_ids, parent_order).reshape(-1)
    own_live = lax.dynamic_index_in_dim(live_slots, myself, 0, keepdims=False)
    own_rows = lax.dynamic_index_in_dim(row_ids, myself, 0, keepdims=False)
    own_parent = lax.dynamic_index_in_dim(parents, myself, 0, keepdims=False)
    leaf_list = []
    parent_list = []
    previous = None
    for tick_index in range(TICKS):
        sources = leaf_sources[0, 0, tick_index]
        interface = None
        if tick_index > 0:
            interface = passed_along(previous[leaf_order - iface_rows :], "panel", 1)
        partial_solution = product(inverse, sources)
        if interface is not None:
            partial_solution = partial_solution + product(inverse, product(coupling, interface))
        update = jnp.where(own_live[:, None], product(upward, partial_solution), 0.0)
        everyone = lax.all_gather(update, "front", axis=0, tiled=True)
        assembled = jax.ops.segment_sum(everyone, targets, num_segments=parent_order + 1)[
            :parent_order
        ]
        solved = product(parent_inverse, parent_sources[0, 0, tick_index] - assembled)
        all_parents = lax.all_gather(solved, "front", axis=0, tiled=True)
        take_index = own_parent * parent_order + own_rows
        picked = jnp.where(own_live[:, None], jnp.take(all_parents, take_index, axis=0), 0.0)
        leaf_now = partial_solution - product(downward, picked)
        leaf_list.append(leaf_now)
        parent_list.append(solved)
        previous = leaf_now
    leaf_out = jnp.stack(leaf_list, axis=0)[None, None]
    parent_out = jnp.stack(parent_list, axis=0)[None, None]
    return (leaf_out, parent_out)


def solution(mesh):
    placed = (
        P("panel", "front", None, None),
        P("panel", "front", None, None),
        P("panel", "front", None, None),
        P("panel", "front", None, None),
        P("panel", "front", None, None),
        P("panel", "front", None, None, None),
        P("panel", "front", None, None, None),
        P("panel", None),
        P("panel", None),
        P("panel", None, None),
    )
    return jax.shard_map(
        local,
        mesh=mesh,
        in_specs=placed,
        out_specs=(P("panel", "front", None, None, None), P("panel", "front", None, None, None)),
        check_vma=False,
    )
```

profile of v0, /device:TPU:1, one launch (start us, length us, event | category | flops | bytes accessed | tf_op | source)
XLA Modules:
  0.0 501.0 jit_solution(5184536901057421567)
XLA Ops:
  8.9 3.1 fusion.14
  16.0 43.4 %all-gather.7.cloned.1.call-done = f32[6144,128]{1,0:T(8,128)} async-done(((f32[384,128]{1,0:T(8,128)}), f32[6144,128]{1,0:T(8,128)}) %all-gather.7.cloned.1.call-update) | async-done | bytes 3145744 | tf_op jit(solution)/shard_map/all_gather | solution.py:64
  59.4 43.9 %scatter_custom_fusion = f32[769,128]{1,0:T(8,128)} fusion(s32[6144]{0:T(1024)} %bitcast.157, f32[6144,128]{1,0:T(8,128)} %all-gather.7.cloned.1.call-done, f32[]{:T(128)} %constant.34.clone.1), kind=kCustom, calls=%fused_computation.73 | custom fusion | flops 786432 | bytes 394240 | tf_op jit(solution)/shard_map/scatter-add | solution.py:65
  103.3 4.8 fusion.4
  110.2 42.6 %all-gather.9.cloned.1.call-done = f32[12288,128]{0,1:T(8,128)} async-done(((f32[768,128]{0,1:T(8,128)}), f32[12288,128]{0,1:T(8,128)}) %all-gather.9.cloned.1.call-update) | async-done | bytes 6291472 | tf_op jit(solution)/shard_map/all_gather | solution.py:69
  152.8 6.6 %copy.12 = f32[12288,128]{1,0:T(8,128)} copy(f32[12288,128]{0,1:T(8,128)} %all-gather.9.cloned.1.call-done) | data formatting | bytes 12582912 | tf_op jit(solution)/shard_map/all_gather | solution.py:69
  159.4 4.4 gather_fusion
  167.2 3.4 collective-permute-start
  170.7 3.0 fusion.12
  181.9 41.1 %all-gather.11.cloned.1.call-done = f32[6144,128]{1,0:T(8,128)} async-done(((f32[384,128]{1,0:T(8,128)}), f32[6144,128]{1,0:T(8,128)}) %all-gather.11.cloned.1.call-update) | async-done | bytes 3145744 | tf_op jit(solution)/shard_map/all_gather | solution.py:64
  223.0 43.9 %scatter_custom_fusion.1 = f32[769,128]{1,0:T(8,128)} fusion(s32[6144]{0:T(1024)} %bitcast.158, f32[6144,128]{1,0:T(8,128)} %all-gather.11.cloned.1.call-done, f32[]{:T(128)} %constant.34.clone.1), kind=kCustom, calls=%fused_computation.71 | custom fusion | flops 786432 | bytes 394240 | tf_op jit(solution)/shard_map/scatter-add | solution.py:65
  267.0 4.8 fusion.2
  272.1 44.4 %all-gather.13.cloned.1.call-done = f32[12288,128]{0,1:T(8,128)} async-done(((f32[768,128]{0,1:T(8,128)}), f32[12288,128]{0,1:T(8,128)}) %all-gather.13.cloned.1.call-update) | async-done | bytes 6291472 | tf_op jit(solution)/shard_map/all_gather | solution.py:69
  316.5 6.6 %copy.15 = f32[12288,128]{1,0:T(8,128)} copy(f32[12288,128]{0,1:T(8,128)} %all-gather.13.cloned.1.call-done) | data formatting | bytes 12582912 | tf_op jit(solution)/shard_map/all_gather | solution.py:69
  323.0 4.4 gather_fusion.1
  327.4 2.7 fusion.28
  330.9 3.3 collective-permute-start.1
  334.1 3.0 fusion.8
  345.6 41.1 %all-gather.15.cloned.1.call-done = f32[6144,128]{1,0:T(8,128)} async-done(((f32[384,128]{1,0:T(8,128)}), f32[6144,128]{1,0:T(8,128)}) %all-gather.15.cloned.1.call-update) | async-done | bytes 3145744 | tf_op jit(solution)/shard_map/all_gather | solution.py:64
  386.7 43.5 %scatter_custom_fusion.2 = f32[769,128]{1,0:T(8,128)S(1)} fusion(s32[6144]{0:T(1024)} %bitcast.159, f32[6144,128]{1,0:T(8,128)} %all-gather.15.cloned.1.call-done, f32[]{:T(128)} %constant.34.clone.1), kind=kCustom, calls=%fused_computation.69 | custom fusion | flops 786432 | bytes 394240 | tf_op jit(solution)/shard_map/scatter-add | solution.py:65
  430.2 4.7 fusion
  437.6 42.0 %all-gather.17.cloned.1.call-done = f32[12288,128]{0,1:T(8,128)} async-done(((f32[768,128]{0,1:T(8,128)}), f32[12288,128]{0,1:T(8,128)}) %all-gather.17.cloned.1.call-update) | async-done | bytes 6291472 | tf_op jit(solution)/shard_map/all_gather | solution.py:69
  479.6 6.6 %copy.18 = f32[12288,128]{1,0:T(8,128)} copy(f32[12288,128]{0,1:T(8,128)} %all-gather.17.cloned.1.call-done) | data formatting | bytes 12582912 | tf_op jit(solution)/shard_map/all_gather | solution.py:69
  486.2 4.5 gather_fusion.2
  (65 shorter events, 35.0 us)
Async XLA Ops:
  7.2 1.7 copy-start
  7.2 52.2 %all-gather.7.cloned.1.call-start = ((), (), s32[]{:S(2)}) async-start(), calls=%async_computation | async-start | bytes 3342336 | tf_op jit(solution)/shard_map/all_gather | solution.py:64
  8.9 3.8 copy-start.1
  11.9 0.7 copy-start.5
  14.5 138.3 %all-gather.9.cloned.1.call-start = ((), (), s32[]{:S(2)}) async-start(), calls=%async_computation.1 | async-start | bytes 6684672 | tf_op jit(solution)/shard_map/all_gather | solution.py:69
  103.3 4.9 copy-start.12
  108.1 114.9 %all-gather.11.cloned.1.call-start = ((), (), s32[]{:S(2)}) async-start(), calls=%async_computation.2 | async-start | bytes 3342336 | tf_op jit(solution)/shard_map/all_gather | solution.py:64
  166.4 0.8 copy-start.8
  167.2 8.6 %copy-start.3 = (f32[1,1,768,512]{3,2,1,0:T(8,128)S(1)}, f32[1,1,768,512]{3,2,1,0:T(8,128)}, u32[]{:S(2)}) copy-start(f32[1,1,768,512]{3,2,1,0:T(8,128)} %param.16) | copy-start | bytes 4718596
  167.2 8.6 %collective-permute-start = (f32[512,128]{1,0:T(8,128)S(1)}, f32[512,128]{1,0:T(8,128)S(1)}, u32[]{:S(2)}, u32[]{:S(2)}) collective-permute-start(f32[512,128]{1,0:T(8,128)S(1)} %slice.51), channel_id=1, source_target_pairs={{0,16},{16,32},{32,48},{48,64},{64,80},{80,96},{96,112},{112,128},... | collective-permute-start | bytes 786440 | tf_op jit(solution)/shard_map/ppermute | solution.py:13
  179.3 0.7 copy-start.7
  181.9 134.6 %all-gather.13.cloned.1.call-start = ((), (), s32[]{:S(2)}) async-start(), calls=%async_computation.3 | async-start | bytes 6684672 | tf_op jit(solution)/shard_map/all_gather | solution.py:69
  271.8 114.9 %all-gather.15.cloned.1.call-start = ((), (), s32[]{:S(2)}) async-start(), calls=%async_computation.4 | async-start | bytes 3342336 | tf_op jit(solution)/shard_map/all_gather | solution.py:64
  330.1 0.7 copy-start.10
  330.9 8.6 %copy-start.4 = (f32[1,1,768,512]{3,2,1,0:T(8,128)S(1)}, f32[1,1,768,512]{3,2,1,0:T(8,128)}, u32[]{:S(2)}) copy-start(f32[1,1,768,512]{3,2,1,0:T(8,128)} %param.16) | copy-start | bytes 4718596
  330.9 8.6 %collective-permute-start.1 = (f32[512,128]{1,0:T(8,128)S(1)}, f32[512,128]{1,0:T(8,128)S(1)}, u32[]{:S(2)}, u32[]{:S(2)}) collective-permute-start(f32[512,128]{1,0:T(8,128)S(1)} %slice.53), channel_id=1, source_target_pairs={{0,16},{16,32},{32,48},{48,64},{64,80},{80,96},{96,112},{112,128},... | collective-permute-start | bytes 786440 | tf_op jit(solution)/shard_map/ppermute | solution.py:13
  343.0 0.7 copy-start.6
  345.5 134.1 %all-gather.17.cloned.1.call-start = ((), (), s32[]{:S(2)}) async-start(), calls=%async_computation.5 | async-start | bytes 6684672 | tf_op jit(solution)/shard_map/all_gather | solution.py:69
  486.1 4.5 copy-start.2
  490.6 2.4 copy-start.9
  490.6 2.4 copy-start.11
Sparse Core Ops, SparseCore 0:
  14.6 44.7 all-gather.6
  108.2 44.5 all-gather.8
  182.0 40.9 all-gather.10
  271.9 44.5 all-gather.12
  345.6 41.0 all-gather.14
  435.0 44.5 all-gather.16
where the time goes:
time: 502 us; the launch traced here: 501 us
  waiting for transfers between devices  259 us (52%)
  other arithmetic  138 us (27%)
  matrix products  43.2 us (9%)
  local copies, waits for them, and re-layouts  39 us (8%)
  between operations  14.3 us (3%)
  starting transfers between devices  7.16 us (1%)
    scatter-add x3, other arithmetic, local(): jax.ops.segment_sum(everyone, targets, num_segments=parent_order + 1)  131 us
    all_gather x3, waiting for transfers between devices, local(): all_parents = lax.all_gather(solved, 'front', axis=0, tiled=True)  129 us
    all_gather x3, waiting for transfers between devices, local(): everyone = lax.all_gather(update, 'front', axis=0, tiled=True)  126 us
    dot_general x16, matrix products, product(): jnp.dot(matrix, operand, precision=highest_precision, preferred_element_t...  43.2 us
    all_gather x3, local copies, waits for them, and re-layouts, local(): all_parents = lax.all_gather(solved, 'front', axis=0, tiled=True)  19.7 us
    gather x3, local copies, waits for them, and re-layouts, local(): jnp.take(all_parents, take_index, axis=0)  13.3 us
  transfers between devices with their start and end apart: 8, of which 8 were waited for; matrix products, arithmetic and copies ran while one was open for 2% of the time, Pallas kernels for 0%

commit v1 on v0

--- a/solution.py
+++ b/solution.py
@@ -66,7 +66,10 @@
             :parent_order
         ]
         solved = product(parent_inverse, parent_sources[0, 0, tick_index] - assembled)
-        all_parents = lax.all_gather(solved, "front", axis=0, tiled=True)
+        devices = lax.axis_size("front")
+        blocks = jnp.stack([solved for _ in range(devices)])
+        blocks = lax.all_to_all(blocks, "front", split_axis=0, concat_axis=0)
+        all_parents = jnp.concatenate(blocks, axis=0)
         take_index = own_parent * parent_order + own_rows
         picked = jnp.where(own_live[:, None], jnp.take(all_parents, take_index, axis=0), 0.0)
         leaf_now = partial_solution - product(downward, picked)

time: 502 us -> 798 us (1.59)
  blocking collectives: 0 us -> 145 us
  waiting for transfers between devices: 259 us -> 400 us
  starting transfers between devices: 7.16 us -> 16.8 us
    all_to_all x0 -> x2, waiting for transfers between devices: none -> 271 us  [local(): blocks = lax.all_to_all(blocks, 'front', split_axis=0, concat_axis=0)]
    all_to_all x0 -> x1, blocking collectives: none -> 145 us  [local(): blocks = lax.all_to_all(blocks, 'front', split_axis=0, concat_axis=0)]
    all_gather x3 -> x0, waiting for transfers between devices: 129 us -> none  [local(): all_parents = lax.all_gather(solved, 'front', axis=0, tiled=True)]
    all_gather x3 -> x0, local copies, waits for them, and re-layouts: 19.7 us -> none  [local(): all_parents = lax.all_gather(solved, 'front', axis=0, tiled=True)]
    all_to_all x0 -> x2, starting transfers between devices: none -> 9.6 us  [local(): blocks = lax.all_to_all(blocks, 'front', split_axis=0, concat_axis=0)]
    another operation x0 -> x3, local copies, waits for them, and re-layouts: none -> 9.08 us  [local(): blocks = jnp.stack([solved for _ in range(devices)])]
  transfers between devices with their start and end apart: 8 -> 7, of which waited for: 8 -> 7; matrix products, arithmetic and copies ran while one was open for 2% -> 2% of each run, Pallas kernels for 0% -> 0%
where the time goes in v1:
time: 798 us; the launch traced here: 790 us
  waiting for transfers between devices  400 us (50%)
  blocking collectives  145 us (18%)
  other arithmetic  138 us (17%)
  matrix products  42.5 us (5%)
  local copies, waits for them, and re-layouts  33.7 us (4%)
  starting transfers between devices  16.8 us (2%)
  between operations  14.2 us (2%)
    all_to_all x2, waiting for transfers between devices, local(): blocks = lax.all_to_all(blocks, 'front', split_axis=0, concat_axis=0)  271 us
    all_to_all x1, blocking collectives, local(): blocks = lax.all_to_all(blocks, 'front', split_axis=0, concat_axis=0)  145 us
    scatter-add x3, other arithmetic, local(): jax.ops.segment_sum(everyone, targets, num_segments=parent_order + 1)  131 us
    all_gather x3, waiting for transfers between devices, local(): everyone = lax.all_gather(update, 'front', axis=0, tiled=True)  125 us
    dot_general x16, matrix products, product(): jnp.dot(matrix, operand, precision=highest_precision, preferred_element_t...  42.5 us
  transfers between devices with their start and end apart: 7, of which 7 were waited for; matrix products, arithmetic and copies ran while one was open for 2% of the time, Pallas kernels for 0%

profile of v1, /device:TPU:1, one launch (start us, length us, event | category | flops | bytes accessed | tf_op | source)
XLA Modules:
  0.0 789.9 jit_solution(2472480792735925941)
XLA Ops:
  8.9 3.1 fusion.14
  15.9 43.4 %all-gather.4.cloned.1.call-done = f32[6144,128]{1,0:T(8,128)} async-done(((f32[384,128]{1,0:T(8,128)}), f32[6144,128]{1,0:T(8,128)}) %all-gather.4.cloned.1.call-update) | async-done | bytes 3145744 | tf_op jit(solution)/shard_map/all_gather | solution.py:64
  59.4 43.9 %scatter_custom_fusion = f32[769,128]{1,0:T(8,128)} fusion(s32[6144]{0:T(1024)} %bitcast.161, f32[6144,128]{1,0:T(8,128)} %all-gather.4.cloned.1.call-done, f32[]{:T(128)} %constant.34.clone.1), kind=kCustom, calls=%fused_computation.73 | custom fusion | flops 786432 | bytes 394240 | tf_op jit(solution)/shard_map/scatter-add | solution.py:65
  103.3 4.8 fusion.4
  110.0 4.2 stack.22
  114.3 4.8 all-to-all-start
  121.1 136.5 %all-to-all-done = f32[16,768,128]{2,1,0:T(8,128)} async-done(((f32[16,768,128]{2,1,0:T(8,128)}), f32[16,768,128]{2,1,0:T(8,128)}, u32[]{:S(2)}, u32[]{:S(2)}) %all-to-all-start) | async-done | bytes 6291488 | tf_op jit(solution)/shard_map/all_to_all | solution.py:71
  257.6 4.4 gather_fusion
  265.5 3.6 collective-permute-start
  269.1 3.0 fusion.12
  279.3 42.3 %all-gather.6.cloned.1.call-done = f32[6144,128]{1,0:T(8,128)} async-done(((f32[384,128]{1,0:T(8,128)}), f32[6144,128]{1,0:T(8,128)}) %all-gather.6.cloned.1.call-update) | async-done | bytes 3145744 | tf_op jit(solution)/shard_map/all_gather | solution.py:64
  321.6 43.9 %scatter_custom_fusion.1 = f32[769,128]{1,0:T(8,128)} fusion(s32[6144]{0:T(1024)} %bitcast.162, f32[6144,128]{1,0:T(8,128)} %all-gather.6.cloned.1.call-done, f32[]{:T(128)} %constant.34.clone.1), kind=kCustom, calls=%fused_computation.71 | custom fusion | flops 786432 | bytes 394240 | tf_op jit(solution)/shard_map/scatter-add | solution.py:65
  365.6 4.8 fusion.2
  373.9 145.2 %all_to_all.15 = f32[16,768,128]{2,1,0:T(8,128)} all-to-all(f32[16,768,128]{2,1,0:T(8,128)S(1)} %stack.24), channel_id=1, replica_groups=mesh['panel'=16,'front'=16] {'front'}, dimensions={0} | all-to-all | bytes 12582912 | tf_op jit(solution)/shard_map/all_to_all | solution.py:71
  519.1 4.4 gather_fusion.1
  526.9 3.5 collective-permute-start.1
  530.4 3.0 fusion.8
  541.8 39.2 %all-gather.8.cloned.1.call-done = f32[6144,128]{1,0:T(8,128)} async-done(((f32[384,128]{1,0:T(8,128)}), f32[6144,128]{1,0:T(8,128)}) %all-gather.8.cloned.1.call-update) | async-done | bytes 3145744 | tf_op jit(solution)/shard_map/all_gather | solution.py:64
  581.0 43.5 %scatter_custom_fusion.2 = f32[769,128]{1,0:T(8,128)S(1)} fusion(s32[6144]{0:T(1024)} %bitcast.163, f32[6144,128]{1,0:T(8,128)} %all-gather.8.cloned.1.call-done, f32[]{:T(128)} %constant.34.clone.1), kind=kCustom, calls=%fused_computation.69 | custom fusion | flops 786432 | bytes 394240 | tf_op jit(solution)/shard_map/scatter-add | solution.py:65
  624.5 3.9 fusion
  628.6 3.2 stack.26
  631.8 4.8 all-to-all-start.2
  640.5 134.7 %all-to-all-done.2 = f32[16,768,128]{2,1,0:T(8,128)} async-done(((f32[16,768,128]{2,1,0:T(8,128)}), f32[16,768,128]{2,1,0:T(8,128)}, u32[]{:S(2)}, u32[]{:S(2)}) %all-to-all-start.2) | async-done | bytes 6291488 | tf_op jit(solution)/shard_map/all_to_all | solution.py:71
  775.2 4.4 gather_fusion.2
  (68 shorter events, 43.0 us)
Async XLA Ops:
  7.2 1.7 copy-start
  7.2 52.2 %all-gather.4.cloned.1.call-start = ((), (), s32[]{:S(2)}) async-start(), calls=%async_computation.3 | async-start | bytes 3342336 | tf_op jit(solution)/shard_map/all_gather | solution.py:64
  8.9 3.8 copy-start.1
  11.9 0.7 copy-start.7
  114.3 4.8 copy-start.14
  114.3 143.4 %all-to-all-start = ((f32[16,768,128]{2,1,0:T(8,128)}), f32[16,768,128]{2,1,0:T(8,128)}, u32[]{:S(2)}, u32[]{:S(2)}) async-start(f32[16,768,128]{2,1,0:T(8,128)} %stack.22), calls=%async_computation | async-start | bytes 12582912 | tf_op jit(solution)/shard_map/all_to_all | solution.py:71
  119.1 202.6 %all-gather.6.cloned.1.call-start = ((), (), s32[]{:S(2)}) async-start(), calls=%async_computation.4 | async-start | bytes 3342336 | tf_op jit(solution)/shard_map/all_gather | solution.py:64
  264.7 0.8 copy-start.10
  265.5 7.8 copy-start.3
  265.5 7.8 collective-permute-start
  276.7 0.7 copy-start.9
  279.3 301.8 %all-gather.8.cloned.1.call-start = ((), (), s32[]{:S(2)}) async-start(), calls=%async_computation.5 | async-start | bytes 3342336 | tf_op jit(solution)/shard_map/all_gather | solution.py:64
  526.2 0.7 copy-start.12
  526.9 8.9 %copy-start.4 = (f32[1,1,768,512]{3,2,1,0:T(8,128)S(1)}, f32[1,1,768,512]{3,2,1,0:T(8,128)}, u32[]{:S(2)}) copy-start(f32[1,1,768,512]{3,2,1,0:T(8,128)} %param.16) | copy-start | bytes 4718596
  526.9 8.9 %collective-permute-start.1 = (f32[512,128]{1,0:T(8,128)S(1)}, f32[512,128]{1,0:T(8,128)S(1)}, u32[]{:S(2)}, u32[]{:S(2)}) collective-permute-start(f32[512,128]{1,0:T(8,128)S(1)} %slice.53), channel_id=1, source_target_pairs={{0,16},{16,32},{32,48},{48,64},{64,80},{80,96},{96,112},{112,128},... | collective-permute-start | bytes 786440 | tf_op jit(solution)/shard_map/ppermute | solution.py:13
  539.3 0.7 copy-start.8
  631.8 4.8 copy-start.5
  631.8 4.8 copy-start.6
  631.8 143.3 %all-to-all-start.2 = ((f32[16,768,128]{2,1,0:T(8,128)}), f32[16,768,128]{2,1,0:T(8,128)}, u32[]{:S(2)}, u32[]{:S(2)}) async-start(f32[16,768,128]{2,1,0:T(8,128)} %stack.26), calls=%async_computation.2 | async-start | bytes 12582912 | tf_op jit(solution)/shard_map/all_to_all | solution.py:71
  637.8 141.8 %copy-start.2 = (f32[1,1,768,384]{3,2,1,0:T(8,128)S(1)}, f32[1,1,768,384]{3,2,1,0:T(8,128)}, u32[]{:S(2)}) copy-start(f32[1,1,768,384]{3,2,1,0:T(8,128)} %param.15) | copy-start | bytes 3538948
  779.6 2.4 copy-start.11
  779.6 2.4 copy-start.13
Sparse Core Ops, SparseCore 0:
  14.6 44.7 all-gather.3
  279.4 42.2 all-gather.5
  541.9 39.0 all-gather.7
